TPU v7x, 256 devices: a whole 4x4x8 slice. The times are simulated.
256 devices in a mesh: pp: 2 (over x_hi), dp: 8 (over y, core), cp: 16 (over z, x_lo).
Axes of the slice: x: 4 (x_hi: 2, x_lo: 2; x = x_hi * 2 + x_lo), y: 4, z: 8, core: 2. Of those that a mesh axis runs over, the one named last changes fastest.
Arguments:
- tokens: bfloat16 [2, 2048, 3584], P('pp', 'cp'), may hold values from -6 to 6
- out_grad: bfloat16 [2, 2048, 3584], P('pp', 'cp'), may hold values from -6 to 6
- probs: bfloat16 [2, 2048, 8], P('pp', 'cp'), may hold values from 0.019897461 to 0.29882812
- expert_ids: int32 [2, 2048, 8], P('pp', 'cp'), may hold values from 0 to 15, all different within a row; in each aligned block of 128 rows (0 to 127, 128 to 255, ..., all dimensions but the last counted through in order) at most 80 rows name the same one
- w_gate: bfloat16 [2, 16, 1280, 3584], P('pp', 'cp', 'dp'), may hold values from -0.09375 to 0.09375
- w_up: bfloat16 [2, 16, 1280, 3584], P('pp', 'cp', 'dp'), may hold values from -0.09375 to 0.09375
- w_down: bfloat16 [2, 16, 1280, 3584], P('pp', 'cp', 'dp'), may hold values from -0.15625 to 0.15625
Outputs:
- passed_grad: bfloat16 [2, 2048, 3584], P('pp', 'cp', 'dp')
- prob_grad: float32 [2, 2048, 8], P('pp', 'cp')
- gate_grad: bfloat16 [2, 16, 1280, 3584], P('pp', 'cp', 'dp')
- up_grad: bfloat16 [2, 16, 1280, 3584], P('pp', 'cp', 'dp')
- down_grad: bfloat16 [2, 16, 1280, 3584], P('pp', 'cp', 'dp')
Inputs may be any that keep to these rules, and one draw needn't show every extreme that they name: `expert_ids`: in each aligned block of 128 tokens of a section, a token names 8 different experts, and no expert is named by more than 80 tokens of the block; some expert is named by exactly 80 tokens of some block.
All inputs are finite; a program needn't handle non-finite values.
Results may differ from a plain program's by a relative error of at most 0.012.
Values may be sent and summed in bfloat16 or wider, within the bound.
A program may use at most 128 MiB of HBM per device.

v0:
```python
import jax
import jax.numpy as jnp
from jax import lax
from jax.sharding import PartitionSpec as P

CAP_NUM, CAP_DEN = (5, 4)


def body(tokens, out_grad, probs, expert_ids, w_gate, w_up, w_down):
    tok_rows = tokens.shape[1]
    width = tokens.shape[2]
    top_count = probs.shape[2]
    experts = lax.axis_size("cp")
    replicas = lax.axis_size("dp")
    capacity = tok_rows * top_count * CAP_NUM // (CAP_DEN * experts)
    columns = width // replicas
    dp = lax.axis_index("dp")
    me = lax.axis_index("cp")
    own = lax.dynamic_slice_in_dim(jnp.stack([tokens[0], out_grad[0]]), dp * columns, columns, 2)
    blocks = lax.all_gather(own, "cp")
    ids_all = lax.all_gather(expert_ids[0], "cp")
    probs_all = lax.all_gather(probs[0], "cp")
    match = ids_all == me
    has = jnp.any(match, axis=2)
    prob_tok = jnp.sum(jnp.where(match, probs_all.astype(jnp.float32), 0.0), axis=2)
    has_i = has.astype(jnp.int32)
    slot = jnp.cumsum(has_i, axis=1) - has_i
    pick = (slot[:, None, :] == jnp.arange(capacity)[None, :, None]) & has[:, None, :]
    probs_in = jnp.sum(jnp.where(pick, prob_tok[:, None, :], 0.0), axis=2).reshape(-1, 1)
    rows = jnp.einsum(
        "bct,bstd->sbcd", pick.astype(jnp.bfloat16), blocks, preferred_element_type=jnp.float32
    ).astype(jnp.bfloat16)
    total_rows = experts * capacity
    rows = rows.reshape(2 * total_rows, columns)
    full = lax.all_gather(rows, "dp", axis=1, tiled=True)
    rows_in, grads_in = (full[:total_rows], full[total_rows:])
    gate_mat = w_gate[0, 0]
    up_mat = w_up[0, 0]
    down_mat = w_down[0, 0]
    by_feature = (((1,), (1,)), ((), ()))
    by_row = (((0,), (0,)), ((), ()))
    gate_pre = lax.dot_general(rows_in, gate_mat, by_feature, preferred_element_type=jnp.float32)
    up_pre = lax.dot_general(rows_in, up_mat, by_feature, preferred_element_type=jnp.float32)
    grad_proj = lax.dot_general(grads_in, down_mat, by_feature, preferred_element_type=jnp.float32)
    sigma = jax.nn.sigmoid(gate_pre)
    silu_gate = gate_pre * sigma
    hidden = (silu_gate * up_pre).astype(jnp.bfloat16)
    prob_part = jnp.sum(hidden.astype(jnp.float32) * grad_proj, axis=1)
    grad_hidden = probs_in * grad_proj
    grad_gate_pre = (grad_hidden * up_pre * sigma * (1.0 + gate_pre * (1.0 - sigma))).astype(
        jnp.bfloat16
    )
    grad_up_pre = (grad_hidden * silu_gate).astype(jnp.bfloat16)
    scaled_hidden = hidden
    scaled_grad = (probs_in * grads_in).astype(jnp.bfloat16)
    input_part = jnp.dot(grad_gate_pre, gate_mat, preferred_element_type=jnp.float32)
    input_part = (
        input_part + jnp.dot(grad_up_pre, up_mat, preferred_element_type=jnp.float32)
    ).astype(jnp.bfloat16)
    gate_grad = lax.dot_general(
        grad_gate_pre, rows_in, by_row, preferred_element_type=jnp.float32
    ).astype(jnp.bfloat16)
    up_grad = lax.dot_general(
        grad_up_pre, rows_in, by_row, preferred_element_type=jnp.float32
    ).astype(jnp.bfloat16)
    down_grad = lax.dot_general(
        scaled_hidden, scaled_grad, by_row, preferred_element_type=jnp.float32
    ).astype(jnp.bfloat16)
    reduced = lax.psum_scatter(input_part, "dp", scatter_dimension=1, tiled=True)
    back = lax.all_to_all(
        reduced.reshape(experts, capacity, columns), "cp", split_axis=0, concat_axis=0, tiled=True
    )
    back_probs = lax.all_to_all(
        prob_part.reshape(experts, capacity), "cp", split_axis=0, concat_axis=0, tiled=True
    )
    back_probs = lax.psum(back_probs, "dp")
    one_hot = expert_ids[0][:, :, None] == jnp.arange(experts)[None, None, :]
    has_e = jnp.any(one_hot, axis=1).astype(jnp.int32)
    slot_e = jnp.cumsum(has_e, axis=0) - has_e
    pick_e = (slot_e[:, :, None] == jnp.arange(capacity)[None, None, :]) & (has_e[:, :, None] > 0)
    input_sum = jnp.dot(
        pick_e.reshape(tok_rows, total_rows).astype(jnp.bfloat16),
        back.reshape(total_rows, columns),
        preferred_element_type=jnp.float32,
    )
    prob_te = jnp.sum(jnp.where(pick_e, back_probs[None], 0.0), axis=2)
    prob_grad = jnp.sum(jnp.where(one_hot, prob_te[:, None, :], 0.0), axis=2)
    passed = lax.ppermute(input_sum.astype(jnp.bfloat16), "pp", [(1, 0)])
    return (
        passed[None],
        prob_grad[None],
        gate_grad[None, None],
        up_grad[None, None],
        down_grad[None, None],
    )


def solution(mesh):
    in_specs = (
        P("pp", "cp", None),
        P("pp", "cp", None),
        P("pp", "cp", None),
        P("pp", "cp", None),
        P("pp", "cp", "dp", None),
        P("pp", "cp", "dp", None),
        P("pp", "cp", "dp", None),
    )
    out_specs = (
        P("pp", "cp", "dp"),
        P("pp", "cp", None),
        P("pp", "cp", "dp", None),
        P("pp", "cp", "dp", None),
        P("pp", "cp", "dp", None),
    )
    return jax.shard_map(body, mesh=mesh, in_specs=in_specs, out_specs=out_specs, check_vma=False)
```

profile of v0, /device:TPU:2, one launch (start us, length us, event | category | flops | bytes accessed | tf_op | source)
XLA Modules:
  0.0 369.4 jit_solution(6365457031545415939)
XLA Ops:
  7.2 0.0 copy-start
  7.2 0.0 all-gather.6.cloned.1.call-start
  7.3 1.6 copy.35
  8.9 1.6 copy.36
  10.5 0.7 fusion.45
  11.2 0.0 all-gather.6.cloned.1.call-update
  11.2 0.0 all-gather.4.cloned.1.call-start
  11.3 33.8 %all_gather.16 = bf16[16,128,8]{1,2,0:T(8,128)(2,1)S(1)} all-gather(bf16[1,128,8]{1,2,0:T(8,128)(2,1)S(1)} %copy-done.4), channel_id=1, replica_groups=mesh['pp'=2,'dp'=8,'cp'=16] {'cp'}, dimensions={0}, use_global_device_ids=true | all-gather | bytes 34816 | tf_op jit(solution)/shard_map/all_gather | solution.py:22
  45.1 33.9 %all_gather.15 = s32[16,128,8]{1,2,0:T(8,128)S(1)} all-gather(s32[1,128,8]{1,2,0:T(8,128)S(1)} %copy-done.3), channel_id=1, replica_groups=mesh['pp'=2,'dp'=8,'cp'=16] {'cp'}, dimensions={0}, use_global_device_ids=true | all-gather | bytes 69632 | tf_op jit(solution)/shard_map/all_gather | solution.py:21
  79.1 0.3 reduce_window_sum.23
  79.4 25.7 %all-gather.6.cloned.1.call-done = bf16[32,128,448]{1,2,0:T(8,128)(2,1)} async-done(((bf16[2,128,448]{1,2,0:T(8,128)(2,1)}), bf16[32,128,448]{1,2,0:T(8,128)(2,1)}) %all-gather.6.cloned.1.call-update) | async-done | bytes 3670032 | tf_op jit(solution)/shard_map/all_gather | solution.py:20
  105.0 3.7 convert_bitcast_fusion
  108.7 1.7 copy.37
  110.4 4.6 %copy.38 = bf16[2560,448]{0,1:T(8,128)(2,1)} copy(bf16[2560,448]{1,0:T(8,128)(2,1)} %bitcast.46) | data formatting | bytes 4587520 | tf_op jit(solution)/shard_map/reshape | solution.py:34
  115.0 0.0 all-gather.4.cloned.1.call-update
  115.0 0.2 reduce-scatter.2.cloned.1.call-start
  115.3 0.4 select_reduce_fusion.1
  115.6 0.1 mul.45
  115.7 94.2 %all-gather.4.cloned.1.call-done = bf16[2560,3584]{0,1:T(8,128)(2,1)} async-done(((bf16[2560,448]{0,1:T(8,128)(2,1)}), bf16[2560,3584]{0,1:T(8,128)(2,1)}) %all-gather.4.cloned.1.call-update) | async-done | bytes 18350096 | tf_op jit(solution)/shard_map/all_gather | solution.py:35
  210.0 5.4 %fusion.10 = f32[1280,160]{0,1:T(8,128)S(1)} fusion(bf16[2560,3584]{0,1:T(8,128)(2,1)} %all-gather.4.cloned.1.call-done, bf16[1,1,160,3584]{3,2,1,0:T(8,128)(2,1)S(1)} %copy-done.2), kind=kOutput, calls=%fused_computation.12 | convolution fusion | flops 1468006400 | bytes 11141120 | tf_op jit(solution)/shard_map/dot_general | solution.py:43
  215.4 0.0 copy-start.6
  215.4 6.1 %fusion.12 = f32[1280,160]{0,1:T(8,128)S(1)} fusion(bf16[2560,3584]{0,1:T(8,128)(2,1)} %all-gather.4.cloned.1.call-done, bf16[1,1,160,3584]{3,2,1,0:T(8,128)(2,1)S(1)} %copy-done), kind=kOutput, calls=%fused_computation.14 | convolution fusion | flops 1468006400 | bytes 11141120 | tf_op jit(solution)/shard_map/dot_general | solution.py:42
  221.4 0.0 copy-done.5
  221.5 0.4 copy-done.6
  221.9 3.2 multiply_reduce_fusion
  225.1 8.9 %fusion.29 = f32[1280,3584]{0,1:T(8,128)} fusion(bf16[1280,160]{0,1:T(8,128)(2,1)S(1)} %get-tuple-element.9, bf16[1,1,160,3584]{3,2,1,0:T(8,128)(2,1)S(1)} %copy-done), kind=kOutput, calls=%fused_computation.27 | convolution fusion | flops 1468006400 | bytes 19906560 | tf_op jit(solution)/shard_map/dot_general | solution.py:56
  234.0 12.3 %fusion = bf16[1280,3584]{0,1:T(8,128)(2,1)} fusion(f32[1280,3584]{0,1:T(8,128)} %fusion.29, bf16[1280,160]{0,1:T(8,128)(2,1)S(1)} %get-tuple-element.10, bf16[1,1,160,3584]{3,2,1,0:T(8,128)(2,1)S(1)} %copy-done.2), kind=kOutput, calls=%fused_computation.2 | convolution fusion | flops 1477181440 | bytes 29081600 | tf_op jit(solution)/shard_map/dot_general | solution.py:58
  246.3 0.0 reduce-scatter.2.cloned.1.call-update
  246.4 0.1 copy.32
  246.5 0.2 reduce_window_sum.22
  246.7 0.7 all_to_all.12
  247.4 8.5 %all-to-all-start.1 = ((f32[16,1,80]{2,1,0:T(1,128)}), f32[16,1,80]{2,1,0:T(1,128)S(1)}, u32[]{:S(2)}, u32[]{:S(2)}) async-start(f32[16,1,80]{2,1,0:T(1,128)} %all_to_all.12), calls=%async_computation.2 | async-start | bytes 16384 | tf_op jit(solution)/shard_map/all_to_all | solution.py:73
  255.9 0.1 copy.34
  255.9 0.1 copy.33
  256.0 49.9 %reduce-scatter.2.cloned.1.call-done = bf16[1280,448]{0,1:T(8,128)(2,1)} async-done(((bf16[1280,3584]{0,1:T(8,128)(2,1)}), bf16[1280,448]{0,1:T(8,128)(2,1)}) %reduce-scatter.2.cloned.1.call-update) | async-done | bytes 1146896 | tf_op jit(solution)/shard_map/reduce_scatter | solution.py:69
  306.0 2.4 copy.39
  308.4 0.0 all-to-all-done.1
  308.4 8.5 %all-to-all-start = ((bf16[16,80,448]{2,1,0:T(8,128)(2,1)}), bf16[16,80,448]{2,1,0:T(8,128)(2,1)S(1)}, u32[]{:S(2)}, u32[]{:S(2)}) async-start(bf16[16,80,448]{2,1,0:T(8,128)(2,1)} %bitcast.9), calls=%async_computation.1 | async-start | bytes 2621440 | tf_op jit(solution)/shard_map/all_to_all | solution.py:70
  316.9 7.8 %fusion.25 = bf16[1,1,160,3584]{3,2,1,0:T(8,128)(2,1)} fusion(bf16[1280,160]{0,1:T(8,128)(2,1)S(1)} %get-tuple-element.9, bf16[2560,3584]{0,1:T(8,128)(2,1)} %all-gather.4.cloned.1.call-done), kind=kOutput, calls=%fused_computation.21 | convolution fusion | flops 1468579840 | bytes 10731520 | tf_op jit(solution)/shard_map/dot_general | solution.py:60
  324.7 7.8 %fusion.22 = bf16[1,1,160,3584]{3,2,1,0:T(8,128)(2,1)} fusion(bf16[1280,160]{0,1:T(8,128)(2,1)S(1)} %get-tuple-element.10, bf16[2560,3584]{0,1:T(8,128)(2,1)} %all-gather.4.cloned.1.call-done), kind=kOutput, calls=%fused_computation.20 | convolution fusion | flops 1468579840 | bytes 10731520 | tf_op jit(solution)/shard_map/dot_general | solution.py:63
  332.5 7.9 %fusion.21 = bf16[1,1,160,3584]{3,2,1,0:T(8,128)(2,1)} fusion(bf16[1280,160]{0,1:T(8,128)(2,1)S(1)} %copy-done.7, f32[1280]{0:T(1024)S(1)} %mul.45, bf16[2560,3584]{0,1:T(8,128)(2,1)} %all-gather.4.cloned.1.call-done), kind=kOutput, calls=%fused_computation.19 | convolution fusion | flops 1482342400 | bytes 10736640 | tf_op jit(solution)/shard_map/dot_general | solution.py:66
  340.4 12.9 %psum.7 = f32[16,80]{1,0:T(8,128)S(1)} all-reduce(f32[16,80]{1,0:T(8,128)S(1)} %bitcast.51), channel_id=1, replica_groups=mesh['pp'=2,'dp'=8,'cp'=16] {'dp'}, use_global_device_ids=true, to_apply=%region_8.9 | all-reduce | flops 1280 | bytes 10240 | tf_op jit(solution)/shard_map/psum | solution.py:76
  353.4 0.6 fusion.28
  354.0 1.3 collective-permute-start
  355.3 0.3 select_reduce_fusion
  355.6 0.6 select_reduce_fusion.2
  356.2 6.0 %collective-permute-done = bf16[128,448]{0,1:T(8,128)(2,1)S(1)} collective-permute-done((bf16[128,448]{0,1:T(8,128)(2,1)S(1)}, bf16[128,448]{0,1:T(8,128)(2,1)S(1)}, u32[]{:S(2)}, u32[]{:S(2)}) %collective-permute-start) | collective-permute-done | bytes 114720 | tf_op jit(solution)/shard_map/ppermute | solution.py:88
  362.2 0.6 copy.42
  (20 shorter events, 0.1 us)
Async XLA Ops:
  7.2 208.2 %copy-start = (bf16[1,1,160,3584]{3,2,1,0:T(8,128)(2,1)S(1)}, bf16[1,1,160,3584]{3,2,1,0:T(8,128)(2,1)}, u32[]{:S(2)}) copy-start(bf16[1,1,160,3584]{3,2,1,0:T(8,128)(2,1)} %param.11) | copy-start | bytes 3440644
  7.2 4.1 %copy-start.4 = (bf16[1,128,8]{1,2,0:T(8,128)(2,1)S(1)}, bf16[1,128,8]{1,2,0:T(8,128)(2,1)}, u32[]{:S(2)}) copy-start(bf16[1,128,8]{1,2,0:T(8,128)(2,1)} %param.9) | copy-start | bytes 6148
  7.2 37.9 %copy-start.3 = (s32[1,128,8]{1,2,0:T(8,128)S(1)}, s32[1,128,8]{1,2,0:T(8,128)}, u32[]{:S(2)}) copy-start(s32[1,128,8]{1,2,0:T(8,128)} %param.10) | copy-start | bytes 12292
  7.2 97.8 %all-gather.6.cloned.1.call-start = ((), (), s32[]{:S(2)}) async-start(), calls=%async_computation.5 | async-start | bytes 3899392 | tf_op jit(solution)/shard_map/all_gather | solution.py:20
  11.2 198.8 %all-gather.4.cloned.1.call-start = ((), (), s32[]{:S(2)}) async-start(), calls=%async_computation.3 | async-start | bytes 20643840 | tf_op jit(solution)/shard_map/all_gather | solution.py:35
  110.4 99.5 %copy-start.2 = (bf16[1,1,160,3584]{3,2,1,0:T(8,128)(2,1)S(1)}, bf16[1,1,160,3584]{3,2,1,0:T(8,128)(2,1)}, u32[]{:S(2)}) copy-start(bf16[1,1,160,3584]{3,2,1,0:T(8,128)(2,1)} %param.12) | copy-start | bytes 3440644
  115.0 190.9 %reduce-scatter.2.cloned.1.call-start = ((), (), s32[]{:S(2)}) async-start(), calls=%async_computation.4 | async-start | bytes 10321920 | tf_op jit(solution)/shard_map/reduce_scatter | solution.py:69
  209.9 11.5 %copy-start.5 = (bf16[2560,3584]{0,1:T(8,128)(2,1)S(1)}, bf16[2560,3584]{0,1:T(8,128)(2,1)}, u32[]{:S(2)}) copy-start(bf16[2560,3584]{0,1:T(8,128)(2,1)} %all-gather.4.cloned.1.call-done) | copy-start | bytes 55050244
  215.4 6.5 %copy-start.6 = (bf16[1,1,160,3584]{3,2,1,0:T(8,128)(2,1)S(1)}, bf16[1,1,160,3584]{3,2,1,0:T(8,128)(2,1)}, u32[]{:S(2)}) copy-start(bf16[1,1,160,3584]{3,2,1,0:T(8,128)(2,1)} %param.13) | copy-start | bytes 3440644
  247.4 61.0 %all-to-all-start.1 = ((f32[16,1,80]{2,1,0:T(1,128)}), f32[16,1,80]{2,1,0:T(1,128)S(1)}, u32[]{:S(2)}, u32[]{:S(2)}) async-start(f32[16,1,80]{2,1,0:T(1,128)} %all_to_all.12), calls=%async_computation.2 | async-start | bytes 16384 | tf_op jit(solution)/shard_map/all_to_all | solution.py:73
  308.4 45.0 %all-to-all-start = ((bf16[16,80,448]{2,1,0:T(8,128)(2,1)}), bf16[16,80,448]{2,1,0:T(8,128)(2,1)S(1)}, u32[]{:S(2)}, u32[]{:S(2)}) async-start(bf16[16,80,448]{2,1,0:T(8,128)(2,1)} %bitcast.9), calls=%async_computation.1 | async-start | bytes 2621440 | tf_op jit(solution)/shard_map/all_to_all | solution.py:70
  324.7 7.8 %copy-start.7 = (bf16[1280,160]{0,1:T(8,128)(2,1)S(1)}, bf16[1280,160]{0,1:T(8,128)(2,1)}, u32[]{:S(2)}) copy-start(bf16[1280,160]{0,1:T(8,128)(2,1)} %get-tuple-element.6) | copy-start | bytes 1228804
  332.5 30.3 %copy-start.1 = (bf16[1,1,160,3584]{3,2,1,0:T(8,128)(2,1)S(1)}, bf16[1,1,160,3584]{3,2,1,0:T(8,128)(2,1)}, u32[]{:S(2)}) copy-start(bf16[1,1,160,3584]{3,2,1,0:T(8,128)(2,1)} %param.11) | copy-start | bytes 3440644
  354.0 8.2 %collective-permute-start = (bf16[128,448]{0,1:T(8,128)(2,1)S(1)}, bf16[128,448]{0,1:T(8,128)(2,1)S(1)}, u32[]{:S(2)}, u32[]{:S(2)}) collective-permute-start(bf16[128,448]{0,1:T(8,128)(2,1)S(1)} %fusion.28), channel_id=1, source_target_pairs={{128,0},{129,1},{130,2},{131,3},{132,4},{133,5},{134,6},{135,7},{1... | collective-permute-start | bytes 344072 | tf_op jit(solution)/shard_map/ppermute | solution.py:88
Sparse Core Ops, SparseCore 0:
  11.3 93.6 all-gather.5
  115.1 94.7 all-gather.3
  246.5 59.4 reduce-scatter.1
where the time goes:
time: 370 us; the launch traced here: 369 us
  waiting for transfers between devices  176 us (48%)
  blocking collectives  80.7 us (22%)
  matrix products  63.8 us (17%)
  starting transfers between devices  18.6 us (5%)
  local copies, waits for them, and re-layouts  14 us (4%)
  between operations  13.9 us (4%)
    all_gather x1, waiting for transfers between devices, body(): full = lax.all_gather(rows, 'dp', axis=1, tiled=True)  94.2 us
    reduce_scatter x1, waiting for transfers between devices, body(): lax.psum_scatter(input_part, 'dp', scatter_dimension=1, tiled=True)  49.9 us
    all_gather x1, blocking collectives, body(): ids_all = lax.all_gather(expert_ids[0], 'cp')  33.9 us
    all_gather x1, blocking collectives, body(): probs_all = lax.all_gather(probs[0], 'cp')  33.8 us
    all_gather x1, waiting for transfers between devices, body(): blocks = lax.all_gather(own, 'cp')  25.7 us
    psum x1, blocking collectives, body(): back_probs = lax.psum(back_probs, 'dp')  12.9 us
    dot_general x1, matrix products, body(): jnp.dot(grad_up_pre, up_mat, preferred_element_type=jnp.float32)  12.3 us
    dot_general x1, matrix products, body(): jnp.dot(grad_gate_pre, gate_mat, preferred_element_type=jnp.float32)  8.93 us
  transfers between devices with their start and end apart: 6, of which 4 were waited for; matrix products, arithmetic and copies ran while one was open for 8% of the time, Pallas kernels for 0%

commit v1 on v0

--- a/solution.py
+++ b/solution.py
@@ -4,6 +4,28 @@
 from jax.sharding import PartitionSpec as P
 
 CAP_NUM, CAP_DEN = (5, 4)
+
+
+def in_order(pieces, dim):
+    pieces = jnp.moveaxis(pieces, 0, dim)
+    shape = pieces.shape
+    return pieces.reshape(*shape[:dim], shape[dim] * shape[dim + 1], *shape[dim + 2 :])
+
+
+def ring_gather(x, axis, dim):
+    size = lax.axis_size(axis)
+    pairs = [(i, (i + 1) % size) for i in range(size)]
+    back = [(b, a) for a, b in pairs]
+    lower, upper = ([], [])
+    for hop in range(size - 1):
+        if hop % 2 == 0:
+            lower.append(lax.ppermute(lower[-1] if lower else x, axis, pairs))
+        else:
+            upper.append(lax.ppermute(upper[-1] if upper else x, axis, back))
+    blocks = jnp.stack([*lower[::-1], x, *upper])
+    shift = lax.axis_index(axis) - len(lower)
+    blocks = blocks[(jnp.arange(size) - shift) % size]
+    return in_order(blocks, dim)
 
 
 def body(tokens, out_grad, probs, expert_ids, w_gate, w_up, w_down):
@@ -32,7 +54,7 @@
     ).astype(jnp.bfloat16)
     total_rows = experts * capacity
     rows = rows.reshape(2 * total_rows, columns)
-    full = lax.all_gather(rows, "dp", axis=1, tiled=True)
+    full = ring_gather(rows, "dp", 1)
     rows_in, grads_in = (full[:total_rows], full[total_rows:])
     gate_mat = w_gate[0, 0]
     up_mat = w_up[0, 0]

time: 370 us -> 478 us (1.29)
  local copies, waits for them, and re-layouts: 14 us -> 114 us
  other arithmetic: 2.56 us -> 17.4 us
  waiting for transfers between devices: 176 us -> 162 us
  starting transfers between devices: 18.6 us -> 23.9 us
    all_gather x1 -> x0, waiting for transfers between devices: 94.2 us -> none  [body(): full = lax.all_gather(rows, 'dp', axis=1, tiled=True)]
    ppermute x0 -> x7, waiting for transfers between devices: none -> 81.8 us  [the longest x4 81.8 us: ring_gather(): lower.append(lax.ppermute(lower[-1] if lower else x, axis, pairs))]
    slice x0 -> x3, local copies, waits for them, and re-layouts: none -> 35.7 us  [body(): rows_in, grads_in = (full[:total_rows], full[total_rows:])]
    ppermute x0 -> x7, local copies, waits for them, and re-layouts: none -> 28.8 us  [the longest x4 15.8 us: ring_gather(): lower.append(lax.ppermute(lower[-1] if lower else x, axis, pairs))]
    gather x0 -> x3, local copies, waits for them, and re-layouts: none -> 26.4 us  [ring_gather(): blocks = blocks[(jnp.arange(size) - shift) % size]]
    transpose x0 -> x1, other arithmetic: none -> 14.8 us  [in_order(): pieces = jnp.moveaxis(pieces, 0, dim)]
    unnamed x19 -> x46, local copies, waits for them, and re-layouts: 4.3 us -> 13.5 us
    ppermute x0 -> x7, starting transfers between devices: none -> 7.54 us  [the longest x3 7.53 us: ring_gather(): upper.append(lax.ppermute(upper[-1] if upper else x, axis, back))]
  transfers between devices with their start and end apart: 6 -> 12, of which waited for: 4 -> 7; matrix products, arithmetic and copies ran while one was open for 8% -> 10% of each run, Pallas kernels for 0% -> 0%
where the time goes in v1:
time: 478 us; the launch traced here: 476 us
  waiting for transfers between devices  162 us (34%)
  local copies, waits for them, and re-layouts  114 us (24%)
  blocking collectives  81.6 us (17%)
  matrix products  62.6 us (13%)
  starting transfers between devices  23.9 us (5%)
  other arithmetic  17.4 us (4%)
  between operations  14.4 us (3%)
    ppermute x4, waiting for transfers between devices, ring_gather(): lower.append(lax.ppermute(lower[-1] if lower else x, axis, pairs))  81.8 us
    reduce_scatter x1, waiting for transfers between devices, body(): lax.psum_scatter(input_part, 'dp', scatter_dimension=1, tiled=True)  49.1 us
    slice x3, local copies, waits for them, and re-layouts, body(): rows_in, grads_in = (full[:total_rows], full[total_rows:])  35.7 us
    all_gather x1, blocking collectives, body(): ids_all = lax.all_gather(expert_ids[0], 'cp')  34.3 us
    all_gather x1, blocking collectives, body(): probs_all = lax.all_gather(probs[0], 'cp')  33.9 us
    gather x3, local copies, waits for them, and re-layouts, ring_gather(): blocks = blocks[(jnp.arange(size) - shift) % size]  26.4 us
    all_gather x1, waiting for transfers between devices, body(): blocks = lax.all_gather(own, 'cp')  25.5 us
    ppermute x4, local copies, waits for them, and re-layouts, ring_gather(): lower.append(lax.ppermute(lower[-1] if lower else x, axis, pairs))  15.8 us
  transfers between devices with their start and end apart: 12, of which 7 were waited for; matrix products, arithmetic and copies ran while one was open for 10% of the time, Pallas kernels for 0%

profile of v1, /device:TPU:2, one launch (start us, length us, event | category | flops | bytes accessed | tf_op | source)
XLA Modules:
  0.0 476.5 jit_solution(5172758969801948769)
XLA Ops:
  7.2 1.6 copy.49
  8.9 1.6 copy.50
  11.2 33.9 %all_gather.13 = bf16[16,128,8]{1,2,0:T(8,128)(2,1)S(1)} all-gather(bf16[1,128,8]{1,2,0:T(8,128)(2,1)} %param.9), channel_id=1, replica_groups=mesh['pp'=2,'dp'=8,'cp'=16] {'cp'}, dimensions={0}, use_global_device_ids=true | all-gather | bytes 34816 | tf_op jit(solution)/shard_map/all_gather | solution.py:44
  45.1 34.3 %all_gather.12 = s32[16,128,8]{1,2,0:T(8,128)S(1)} all-gather(s32[1,128,8]{1,2,0:T(8,128)} %param.10), channel_id=1, replica_groups=mesh['pp'=2,'dp'=8,'cp'=16] {'cp'}, dimensions={0}, use_global_device_ids=true | all-gather | bytes 69632 | tf_op jit(solution)/shard_map/all_gather | solution.py:43
  79.8 25.5 %all-gather.3.cloned.1.call-done = bf16[32,128,448]{1,2,0:T(8,128)(2,1)} async-done(((bf16[2,128,448]{1,2,0:T(8,128)(2,1)}), bf16[32,128,448]{1,2,0:T(8,128)(2,1)}) %all-gather.3.cloned.1.call-update) | async-done | bytes 3670032 | tf_op jit(solution)/shard_map/all_gather | solution.py:42
  105.3 3.7 convert_bitcast_fusion
  108.9 1.7 copy.51
  110.7 4.5 copy.52
  115.1 3.0 collective-permute-start.4
  118.1 26.0 %collective-permute-done = bf16[2560,448]{0,1:T(8,128)(2,1)S(1)} collective-permute-done((bf16[2560,448]{0,1:T(8,128)(2,1)}, bf16[2560,448]{0,1:T(8,128)(2,1)S(1)}, u32[]{:S(2)}, u32[]{:S(2)}) %collective-permute-start) | collective-permute-done | bytes 2293792 | tf_op jit(solution)/shard_map/ppermute | solution.py:22
  144.1 3.0 collective-permute-start.5
  147.1 25.8 %collective-permute-done.1 = bf16[2560,448]{0,1:T(8,128)(2,1)S(1)} collective-permute-done((bf16[2560,448]{0,1:T(8,128)(2,1)S(1)}, bf16[2560,448]{0,1:T(8,128)(2,1)S(1)}, u32[]{:S(2)}, u32[]{:S(2)}) %collective-permute-start.1) | collective-permute-done | bytes 2293792 | tf_op jit(solution)/shard_map/ppermute | solution.py:22
  172.9 1.4 copy-done.9
  174.3 1.6 collective-permute-start.6
  175.9 25.8 %collective-permute-done.2 = bf16[2560,448]{0,1:T(8,128)(2,1)} collective-permute-done((bf16[2560,448]{0,1:T(8,128)(2,1)S(1)}, bf16[2560,448]{0,1:T(8,128)(2,1)}, u32[]{:S(2)}, u32[]{:S(2)}) %collective-permute-start.2) | collective-permute-done | bytes 2293792 | tf_op jit(solution)/shard_map/ppermute | solution.py:22
  202.2 2.6 copy.56
  204.9 4.3 copy.59
  209.2 4.3 copy.55
  213.6 4.4 copy.60
  217.9 4.4 copy.54
  222.3 4.4 copy.61
  226.7 4.2 collective-permute-done.3
  230.9 4.4 copy.53
  235.3 2.1 bitcast_dynamic-update-slice_fusion.6
  237.3 2.2 bitcast_dynamic-update-slice_fusion.5
  243.2 7.3 %fusion.32 = (bf16[8,1280,448]{2,1,0:T(8,128)(2,1)}, bf16[8,1280,448]{2,1,0:T(8,128)(2,1)}) fusion(bf16[8,2560,448]{2,1,0:T(8,128)(2,1)S(1)} %bitcast_dynamic-update-slice_fusion), kind=kLoop, calls=%fused_computation.70 | loop fusion | bytes 36700160 | tf_op jit(solution)/shard_map/gather | solution.py:27
  250.5 9.5 %gather_fusion = bf16[8,1280,448]{2,1,0:T(8,128)(2,1)} fusion(bf16[8,1280,448]{2,1,0:T(8,128)(2,1)} %get-tuple-element.11, s32[1024]{0:T(1024)S(1)} %pad_clamp_fusion), kind=kCustom, calls=%fused_computation | custom fusion | bytes 18350112 | tf_op jit(solution)/shard_map/gather | solution.py:27
  260.0 9.6 %gather_fusion.1 = bf16[8,1280,448]{2,1,0:T(8,128)(2,1)} fusion(bf16[8,1280,448]{2,1,0:T(8,128)(2,1)} %get-tuple-element.12, s32[1024]{0:T(1024)S(1)} %pad_clamp_fusion), kind=kCustom, calls=%fused_computation.1 | custom fusion | bytes 18350112 | tf_op jit(solution)/shard_map/gather | solution.py:27
  269.6 14.8 %maximum_bitcast_fusion = bf16[2560,8,448]{2,0,1:T(8,128)(2,1)S(1)} fusion(bf16[8,1280,448]{2,1,0:T(8,128)(2,1)} %gather_fusion.1, bf16[8,1280,448]{2,1,0:T(8,128)(2,1)} %gather_fusion), kind=kLoop, calls=%fused_computation.2 | loop fusion | flops 36700160 | bytes 36700160 | tf_op jit(solution)/shard_map/transpose | solution.py:10
  284.4 7.4 %fusion.31 = (bf16[1280,8,448]{2,0,1:T(8,128)(2,1)}, bf16[1280,8,448]{2,0,1:T(8,128)(2,1)}) fusion(bf16[2560,8,448]{2,0,1:T(8,128)(2,1)S(1)} %maximum_bitcast_fusion), kind=kLoop, calls=%fused_computation.69 | loop fusion | bytes 36700160 | tf_op jit(solution)/shard_map/slice | solution.py:58
  291.8 14.1 %copy.63 = bf16[1280,8,448]{0,2,1:T(8,128)(2,1)} copy(bf16[1280,8,448]{2,0,1:T(8,128)(2,1)} %get-tuple-element.10) | data formatting | bytes 18350080 | tf_op jit(solution)/shard_map/slice | solution.py:58
  306.0 6.3 %fusion.10 = f32[1280,160]{0,1:T(8,128)} fusion(bf16[1280,3584]{0,1:T(8,128)(2,1)} %bitcast.72, bf16[1,1,160,3584]{3,2,1,0:T(8,128)(2,1)S(1)} %copy-done), kind=kOutput, calls=%fused_computation.28 | convolution fusion | flops 1468006400 | bytes 11141120 | tf_op jit(solution)/shard_map/dot_general | solution.py:64
  312.8 2.5 fusion.13
  315.3 14.1 %copy.62 = bf16[1280,8,448]{0,2,1:T(8,128)(2,1)} copy(bf16[1280,8,448]{2,0,1:T(8,128)(2,1)} %get-tuple-element.9) | data formatting | bytes 18350080 | tf_op jit(solution)/shard_map/slice | solution.py:58
  329.5 7.0 %multiply_reduce_fusion = (f32[1280]{0:T(1024)S(1)}, bf16[1280,160]{0,1:T(8,128)(2,1)}, bf16[1280,160]{0,1:T(8,128)(2,1)S(1)}, bf16[1280,160]{0,1:T(8,128)(2,1)S(1)}) fusion(f32[1280,160]{0,1:T(8,128)} %fusion.13, f32[1280,160]{0,1:T(8,128)} %fusion.10, f32[1280]{0:T(1024)S(1)} %mul.45, bf16[1280,3584]{0,1:T(8,128)(2,1)} %bitcast.80, ...), kind=kOutput, calls=%fused_computation.35 | convolution fusion | flops 1471896320 | bytes 13199360 | tf_op jit(solution)/shard_map/dot_general | solution.py:66
  336.4 8.8 %fusion.8 = f32[1280,3584]{0,1:T(8,128)} fusion(bf16[1280,160]{0,1:T(8,128)(2,1)S(1)} %get-tuple-element.13, bf16[1,1,160,3584]{3,2,1,0:T(8,128)(2,1)S(1)} %copy-done), kind=kOutput, calls=%fused_computation.26 | convolution fusion | flops 1468006400 | bytes 19906560 | tf_op jit(solution)/shard_map/dot_general | solution.py:78
  345.3 12.5 %fusion = bf16[1280,3584]{0,1:T(8,128)(2,1)} fusion(f32[1280,3584]{0,1:T(8,128)} %fusion.8, bf16[1280,160]{0,1:T(8,128)(2,1)S(1)} %get-tuple-element.14, bf16[1,1,160,3584]{3,2,1,0:T(8,128)(2,1)S(1)} %copy-done.7), kind=kOutput, calls=%fused_computation.5 | convolution fusion | flops 1477181440 | bytes 29081600 | tf_op jit(solution)/shard_map/dot_general | solution.py:80
  358.5 6.5 %all-to-all-start.1 = ((f32[16,1,80]{2,1,0:T(1,128)}), f32[16,1,80]{2,1,0:T(1,128)S(1)}, u32[]{:S(2)}, u32[]{:S(2)}) async-start(f32[16,1,80]{2,1,0:T(1,128)} %all_to_all.12), calls=%async_computation.2 | async-start | bytes 16384 | tf_op jit(solution)/shard_map/all_to_all | solution.py:95
  365.1 49.1 %reduce-scatter.2.cloned.1.call-done = bf16[1280,448]{0,1:T(8,128)(2,1)} async-done(((bf16[1280,3584]{0,1:T(8,128)(2,1)}), bf16[1280,448]{0,1:T(8,128)(2,1)}) %reduce-scatter.2.cloned.1.call-update) | async-done | bytes 1146896 | tf_op jit(solution)/shard_map/reduce_scatter | solution.py:91
  414.2 2.4 copy.64
  416.6 8.5 %all-to-all-start = ((bf16[16,80,448]{2,1,0:T(8,128)(2,1)}), bf16[16,80,448]{2,1,0:T(8,128)(2,1)}, u32[]{:S(2)}, u32[]{:S(2)}) async-start(bf16[16,80,448]{2,1,0:T(8,128)(2,1)} %bitcast.21), calls=%async_computation.1 | async-start | bytes 2621440 | tf_op jit(solution)/shard_map/all_to_all | solution.py:92
  425.5 7.9 %fusion.6 = bf16[1,1,160,3584]{3,2,1,0:T(8,128)(2,1)} fusion(bf16[1280,160]{0,1:T(8,128)(2,1)S(1)} %get-tuple-element.14, bf16[1280,3584]{0,1:T(8,128)(2,1)} %bitcast.73), kind=kOutput, calls=%fused_computation.13 | convolution fusion | flops 1468579840 | bytes 10731520 | tf_op jit(solution)/shard_map/dot_general | solution.py:85
  433.3 7.8 %fusion.5 = bf16[1,1,160,3584]{3,2,1,0:T(8,128)(2,1)} fusion(bf16[1280,160]{0,1:T(8,128)(2,1)S(1)} %get-tuple-element.13, bf16[1280,3584]{0,1:T(8,128)(2,1)} %bitcast.74), kind=kOutput, calls=%fused_computation.12 | convolution fusion | flops 1468579840 | bytes 10731520 | tf_op jit(solution)/shard_map/dot_general | solution.py:82
  441.2 4.2 fusion.4
  445.4 13.4 %psum.7 = f32[16,80]{1,0:T(8,128)S(1)} all-reduce(f32[16,80]{1,0:T(8,128)S(1)} %bitcast.88), channel_id=1, replica_groups=mesh['pp'=2,'dp'=8,'cp'=16] {'dp'}, use_global_device_ids=true, to_apply=%region_8.9 | all-reduce | flops 1280 | bytes 10240 | tf_op jit(solution)/shard_map/psum | solution.py:98
  458.8 1.9 fusion.7
  460.8 1.3 collective-permute-start.7
  463.0 6.0 %collective-permute-done.7 = bf16[128,448]{0,1:T(8,128)(2,1)S(1)} collective-permute-done((bf16[128,448]{0,1:T(8,128)(2,1)S(1)}, bf16[128,448]{0,1:T(8,128)(2,1)S(1)}, u32[]{:S(2)}, u32[]{:S(2)}) %collective-permute-start.7) | collective-permute-done | bytes 114720 | tf_op jit(solution)/shard_map/ppermute | solution.py:110
  (77 shorter events, 8.5 us)
Async XLA Ops:
  7.2 298.8 %copy-start = (bf16[1,1,160,3584]{3,2,1,0:T(8,128)(2,1)S(1)}, bf16[1,1,160,3584]{3,2,1,0:T(8,128)(2,1)}, u32[]{:S(2)}) copy-start(bf16[1,1,160,3584]{3,2,1,0:T(8,128)(2,1)} %param.11) | copy-start | bytes 3440644
  7.2 98.1 %all-gather.3.cloned.1.call-start = ((), (), s32[]{:S(2)}) async-start(), calls=%async_computation.4 | async-start | bytes 3899392 | tf_op jit(solution)/shard_map/all_gather | solution.py:42
  11.2 403.0 %reduce-scatter.2.cloned.1.call-start = ((), (), s32[]{:S(2)}) async-start(), calls=%async_computation.3 | async-start | bytes 10321920 | tf_op jit(solution)/shard_map/reduce_scatter | solution.py:91
  115.1 29.0 %collective-permute-start = (bf16[2560,448]{0,1:T(8,128)(2,1)}, bf16[2560,448]{0,1:T(8,128)(2,1)S(1)}, u32[]{:S(2)}, u32[]{:S(2)}) collective-permute-start(bf16[2560,448]{0,1:T(8,128)(2,1)} %copy.52), channel_id=1, source_target_pairs={{0,16},{16,32},{32,48},{48,64},{64,80},{80,96},{96,112},{112,0},{1... | collective-permute-start | bytes 6881288 | tf_op jit(solution)/shard_map/ppermute | solution.py:22
  115.1 29.0 %collective-permute-start.4 = (bf16[2560,448]{0,1:T(8,128)(2,1)}, bf16[2560,448]{0,1:T(8,128)(2,1)S(1)}, u32[]{:S(2)}, u32[]{:S(2)}) collective-permute-start(bf16[2560,448]{0,1:T(8,128)(2,1)} %copy.52), channel_id=1, source_target_pairs={{16,0},{32,16},{48,32},{64,48},{80,64},{96,80},{112,96},{0,112},{1... | collective-permute-start | bytes 6881288 | tf_op jit(solution)/shard_map/ppermute | solution.py:24
  144.1 28.8 %collective-permute-start.1 = (bf16[2560,448]{0,1:T(8,128)(2,1)S(1)}, bf16[2560,448]{0,1:T(8,128)(2,1)S(1)}, u32[]{:S(2)}, u32[]{:S(2)}) collective-permute-start(bf16[2560,448]{0,1:T(8,128)(2,1)S(1)} %collective-permute-done), channel_id=1, source_target_pairs={{0,16},{16,32},{32,48},{48,64},{64,80},{80,96},{96,112},{112,0},{1... | collective-permute-start | bytes 6881288 | tf_op jit(solution)/shard_map/ppermute | solution.py:22
  144.1 28.8 %copy-start.8 = (bf16[2560,448]{0,1:T(8,128)(2,1)}, bf16[2560,448]{0,1:T(8,128)(2,1)S(1)}, u32[]{:S(2)}) copy-start(bf16[2560,448]{0,1:T(8,128)(2,1)S(1)} %collective-permute-done.4) | copy-start | bytes 6881284
  144.1 28.8 %collective-permute-start.5 = (bf16[2560,448]{0,1:T(8,128)(2,1)S(1)}, bf16[2560,448]{0,1:T(8,128)(2,1)}, u32[]{:S(2)}, u32[]{:S(2)}) collective-permute-start(bf16[2560,448]{0,1:T(8,128)(2,1)S(1)} %collective-permute-done.4), channel_id=1, source_target_pairs={{16,0},{32,16},{48,32},{64,48},{80,64},{96,80},{112,96},{0,112},{1... | collective-permute-start | bytes 6881288 | tf_op jit(solution)/shard_map/ppermute | solution.py:24
  172.9 1.4 copy-start.9
  172.9 28.9 %collective-permute-start.2 = (bf16[2560,448]{0,1:T(8,128)(2,1)S(1)}, bf16[2560,448]{0,1:T(8,128)(2,1)}, u32[]{:S(2)}, u32[]{:S(2)}) collective-permute-start(bf16[2560,448]{0,1:T(8,128)(2,1)S(1)} %collective-permute-done.1), channel_id=1, source_target_pairs={{0,16},{16,32},{32,48},{48,64},{64,80},{80,96},{96,112},{112,0},{1... | collective-permute-start | bytes 6881288 | tf_op jit(solution)/shard_map/ppermute | solution.py:22
  174.3 48.0 %collective-permute-start.6 = (bf16[2560,448]{0,1:T(8,128)(2,1)}, bf16[2560,448]{0,1:T(8,128)(2,1)}, u32[]{:S(2)}, u32[]{:S(2)}) collective-permute-start(bf16[2560,448]{0,1:T(8,128)(2,1)} %collective-permute-done.5), channel_id=1, source_target_pairs={{16,0},{32,16},{48,32},{64,48},{80,64},{96,80},{112,96},{0,112},{1... | collective-permute-start | bytes 6881288 | tf_op jit(solution)/shard_map/ppermute | solution.py:24
  201.8 29.1 %collective-permute-start.3 = (bf16[2560,448]{0,1:T(8,128)(2,1)}, bf16[2560,448]{0,1:T(8,128)(2,1)}, u32[]{:S(2)}, u32[]{:S(2)}) collective-permute-start(bf16[2560,448]{0,1:T(8,128)(2,1)} %collective-permute-done.2), channel_id=1, source_target_pairs={{0,16},{16,32},{32,48},{48,64},{64,80},{80,96},{96,112},{112,0},{1... | collective-permute-start | bytes 6881288 | tf_op jit(solution)/shard_map/ppermute | solution.py:22
  235.3 4.3 copy-start.6
  235.3 4.5 copy-start.4
  237.3 3.1 copy-start.1
  239.6 1.9 copy-start.2
  239.8 2.5 copy-start.3
  239.9 3.0 copy-start.5
  306.0 6.3 %slice-start = ((s8[9175040]{0:T(1024)(128)(4,1)}), s8[4194304]{0:T(1024)(128)(4,1)S(1)}, s32[]{:S(2)}) async-start(s8[9175040]{0:T(1024)(128)(4,1)} %bitcast.75), calls=%async_computation.5 | async-start | bytes 8388608
  306.0 6.3 %copy-start.7 = (bf16[1,1,160,3584]{3,2,1,0:T(8,128)(2,1)S(1)}, bf16[1,1,160,3584]{3,2,1,0:T(8,128)(2,1)}, u32[]{:S(2)}) copy-start(bf16[1,1,160,3584]{3,2,1,0:T(8,128)(2,1)} %param.12) | copy-start | bytes 3440644
  306.0 6.4 %slice-start.1 = ((s8[9175040]{0:T(1024)(128)(4,1)}), s8[4194304]{0:T(1024)(128)(4,1)S(1)}, s32[]{:S(2)}) async-start(s8[9175040]{0:T(1024)(128)(4,1)} %bitcast.75), calls=%async_computation.6 | async-start | bytes 8388608
  306.0 6.8 %slice-start.2 = ((s8[9175040]{0:T(1024)(128)(4,1)}), s8[786432]{0:T(1024)(128)(4,1)S(1)}, s32[]{:S(2)}) async-start(s8[9175040]{0:T(1024)(128)(4,1)} %bitcast.75), calls=%async_computation.7 | async-start | bytes 1572864
  357.8 7.2 %copy-start.10 = (s32[1,128,8]{1,2,0:T(8,128)S(1)}, s32[1,128,8]{1,2,0:T(8,128)}, u32[]{:S(2)}) copy-start(s32[1,128,8]{1,2,0:T(8,128)} %param.10) | copy-start | bytes 12292
  358.5 58.1 %all-to-all-start.1 = ((f32[16,1,80]{2,1,0:T(1,128)}), f32[16,1,80]{2,1,0:T(1,128)S(1)}, u32[]{:S(2)}, u32[]{:S(2)}) async-start(f32[16,1,80]{2,1,0:T(1,128)} %all_to_all.12), calls=%async_computation.2 | async-start | bytes 16384 | tf_op jit(solution)/shard_map/all_to_all | solution.py:95
  416.6 42.2 %all-to-all-start = ((bf16[16,80,448]{2,1,0:T(8,128)(2,1)}), bf16[16,80,448]{2,1,0:T(8,128)(2,1)}, u32[]{:S(2)}, u32[]{:S(2)}) async-start(bf16[16,80,448]{2,1,0:T(8,128)(2,1)} %bitcast.21), calls=%async_computation.1 | async-start | bytes 2621440 | tf_op jit(solution)/shard_map/all_to_all | solution.py:92
  425.4 15.7 %slice-start.3 = ((s8[9175040]{0:T(1024)(128)(4,1)}), s8[4194304]{0:T(1024)(128)(4,1)S(1)}, s32[]{:S(2)}) async-start(s8[9175040]{0:T(1024)(128)(4,1)} %bitcast.81), calls=%async_computation.8 | async-start | bytes 8388608
  425.4 15.7 %slice-start.4 = ((s8[9175040]{0:T(1024)(128)(4,1)}), s8[4194304]{0:T(1024)(128)(4,1)S(1)}, s32[]{:S(2)}) async-start(s8[9175040]{0:T(1024)(128)(4,1)} %bitcast.81), calls=%async_computation.9 | async-start | bytes 8388608
  425.4 15.7 %copy-start.11 = (bf16[1280,160]{0,1:T(8,128)(2,1)S(1)}, bf16[1280,160]{0,1:T(8,128)(2,1)}, u32[]{:S(2)}) copy-start(bf16[1280,160]{0,1:T(8,128)(2,1)} %get-tuple-element.6) | copy-start | bytes 1228804
  433.3 7.8 %slice-start.5 = ((s8[9175040]{0:T(1024)(128)(4,1)}), s8[786432]{0:T(1024)(128)(4,1)S(1)}, s32[]{:S(2)}) async-start(s8[9175040]{0:T(1024)(128)(4,1)} %bitcast.81), calls=%async_computation.10 | async-start | bytes 1572864
  460.8 8.2 %collective-permute-start.7 = (bf16[128,448]{0,1:T(8,128)(2,1)S(1)}, bf16[128,448]{0,1:T(8,128)(2,1)S(1)}, u32[]{:S(2)}, u32[]{:S(2)}) collective-permute-start(bf16[128,448]{0,1:T(8,128)(2,1)S(1)} %fusion.7), channel_id=1, source_target_pairs={{128,0},{129,1},{130,2},{131,3},{132,4},{133,5},{134,6},{135,7},{1... | collective-permute-start | bytes 344072 | tf_op jit(solution)/shard_map/ppermute | solution.py:110
Sparse Core Ops, SparseCore 0:
  11.3 93.9 all-gather.2
  357.9 56.2 reduce-scatter.1
